TPU v7x, 32 devices: a whole 2x2x4 slice. The times are simulated.
32 devices in a mesh: rep: 2 (over x), shard: 16 (over z, y, core).
Axes of the slice: x: 2, y: 2, z: 4, core: 2. Of those that a mesh axis runs over, the one named last changes fastest.
Arguments:
- features: bfloat16 [1, 2, 2048, 8192], P(None, 'rep', 'shard'), may hold values from -6 to 6
- out_grads: bfloat16 [1, 2, 2048, 1024], P(None, 'rep', 'shard'), may hold values from -6 to 6
- doc_ids: int32 [1, 2, 2048], P(None, 'rep', 'shard'), may hold values from 0 to 15, never falling along the last dimension, each value on 1 to 256 neighbouring positions
- offsets: int32 [1, 16, 128], P(None, None, 'shard'), may hold values from 0 to 15
- momentum: bfloat16 [2, 1024, 8192], P('rep', None, 'shard'), may hold values from -6 to 6
Outputs:
- residual_momentum: bfloat16 [2, 1024, 8192], P('rep', None, 'shard')
- update: bfloat16 [1, 1024, 8192], P(None, None, 'shard')
Inputs may be any that keep to these rules, and one draw needn't show every extreme that they name: `doc_ids`: along each step's and group's tokens the document number never falls; every number from 0 to 15 occurs, none more than 256 times.
All inputs are finite; a program needn't handle non-finite values.
Results may differ from a plain program's by a relative error of at most 0.012.
Values may be sent and summed in bfloat16 or wider, within the bound.
A program may use at most 64 MiB of HBM per device.

v0:
```python
import math

import jax
import jax.numpy as jnp
from jax import lax
from jax.sharding import PartitionSpec as P

BLOCK = 64
STRIDE = 16
DOCS = 16


BETA = 0.9
CLIP = 2.0
EPS = 1e-06
PRECISE = lax.Precision.HIGHEST


def dct_table(size):
    freq = lax.broadcasted_iota(jnp.float32, (size, size), 0)
    place = lax.broadcasted_iota(jnp.float32, (size, size), 1)
    matrix = jnp.cos(math.pi * (2.0 * place + 1.0) * freq / (2.0 * size)) * math.sqrt(2.0 / size)
    return jnp.where(freq == 0, matrix / math.sqrt(2.0), matrix)


def forward(moment, matrix, matrix_pair):
    shaped = moment.reshape(-1, BLOCK, moment.shape[1])
    mixed = jnp.einsum("ku,aud->akd", matrix, shaped, precision=PRECISE)
    flat = mixed.reshape(-1, 2 * BLOCK)
    return jnp.dot(flat, matrix_pair.T, precision=PRECISE).reshape(moment.shape)


def inverse(spectrum, matrix, matrix_pair):
    shaped = spectrum.reshape(-1, BLOCK, spectrum.shape[1])
    mixed = jnp.einsum("ku,akd->aud", matrix, shaped, precision=PRECISE)
    flat = mixed.reshape(-1, 2 * BLOCK)
    return jnp.dot(flat, matrix_pair, precision=PRECISE).reshape(spectrum.shape)


def selector_for(offsets_step):
    grouped = jnp.repeat(offsets_step, BLOCK // STRIDE, axis=1)
    row_index = jnp.arange(BLOCK, dtype=jnp.int32)
    shift_amount = (grouped[:, None, :] - row_index[None, :, None]) % STRIDE
    residue = jnp.arange(STRIDE, dtype=jnp.int32)
    return (residue == shift_amount[..., None]).astype(jnp.float32)


def pack_entries(spectrum, selector):
    shaped = spectrum.reshape(-1, BLOCK, spectrum.shape[1] // STRIDE, STRIDE)
    return jnp.sum(shaped * selector, axis=-1)


def place_entries(packed, selector, row_count, row_width):
    return (packed[..., None] * selector).reshape(row_count, row_width)


def expand_scale(block_scale):
    return jnp.repeat(block_scale.astype(jnp.float32), BLOCK // STRIDE, axis=-1)[..., None, :]


def body(features, out_grads, doc_ids, offsets, momentum):
    matrix = dct_table(BLOCK)
    matrix_pair = jnp.kron(jnp.eye(2, dtype=jnp.float32), matrix)
    local_docs = doc_ids[:, 0, :]
    onehot = (local_docs[:, :, None] == jnp.arange(DOCS, dtype=jnp.int32)).astype(jnp.float32)
    lengths = lax.psum(jnp.sum(onehot, axis=1), "shard")
    token_weight = jnp.sum(onehot / lengths[:, None, :], axis=2)
    scaled = (out_grads[:, 0].astype(jnp.float32) * token_weight[:, :, None]).astype(jnp.bfloat16)
    moment = momentum[0].astype(jnp.float32)
    rows_here, row_width = moment.shape
    step_rows = features[0, 0]
    step_grads = scaled[0]
    columns = lax.all_to_all(step_rows, "shard", split_axis=1, concat_axis=0, tiled=True)
    every_grad = lax.all_gather(step_grads, "shard", axis=0, tiled=True)
    summed = lax.dot_general(
        every_grad, columns, (((0,), (0,)), ((), ())), preferred_element_type=jnp.float32
    )
    gradient = summed.astype(jnp.bfloat16)
    moment = BETA * moment + gradient.astype(jnp.float32)
    spectrum = forward(moment, matrix, matrix_pair)
    selector = selector_for(offsets[0])
    packed = pack_entries(spectrum, selector)
    shaped = packed.reshape(packed.shape[0], BLOCK, row_width // BLOCK, BLOCK // STRIDE)
    mean_square = jnp.mean(shaped * shaped, axis=(1, 3))
    block_scale = (CLIP * jnp.sqrt(mean_square + EPS)).astype(jnp.bfloat16)
    spread = expand_scale(block_scale)
    quantized = jnp.clip(packed / spread, -1.0, 1.0).astype(jnp.bfloat16)
    decoded = quantized.astype(jnp.float32) * spread
    moment = moment - inverse(
        place_entries(decoded, selector, rows_here, row_width), matrix, matrix_pair
    )
    gathered_values = lax.all_gather(quantized[None], "rep", axis=0, tiled=True)
    gathered_scales = lax.all_gather(block_scale[None], "rep", axis=0, tiled=True)
    group_total = jnp.sum(
        gathered_values.astype(jnp.float32) * expand_scale(gathered_scales), axis=0
    )
    average = group_total / lax.axis_size("rep")
    update_step = inverse(
        place_entries(average, selector, rows_here, row_width), matrix, matrix_pair
    )
    updates = [update_step.astype(jnp.bfloat16)]
    return (moment.astype(jnp.bfloat16)[None], jnp.stack(updates))


def solution(mesh):
    return jax.shard_map(
        body,
        mesh=mesh,
        in_specs=(
            P(None, "rep", "shard", None),
            P(None, "rep", "shard", None),
            P(None, "rep", "shard"),
            P(None, None, "shard"),
            P("rep", None, "shard"),
        ),
        out_specs=(P("rep", None, "shard"), P(None, None, "shard")),
        check_vma=False,
    )
```

profile of v0, /device:TPU:14, one launch (start us, length us, event | category | flops | bytes accessed | tf_op | source)
XLA Modules:
  0.0 217.7 jit_solution(13524638102951302133)
XLA Ops:
  7.2 0.8 convert_reduce_fusion
  8.0 21.1 %psum.7 = f32[16]{0:T(128)S(1)} all-reduce(f32[16]{0:T(128)S(1)} %convert_reduce_fusion), channel_id=1, replica_groups=mesh['rep'=2,'shard'=16] {'shard'}, use_global_device_ids=true, to_apply=%region_1.2 | all-reduce | flops 16 | bytes 128 | tf_op jit(solution)/shard_map/psum | solution.py:66
  29.0 0.7 fusion.11
  29.8 1.8 fusion.2
  31.6 4.1 %copy.62 = bf16[1,1,128,8192]{2,3,1,0:T(8,128)(2,1)} copy(bf16[1,1,128,8192]{3,2,1,0:T(8,128)(2,1)} %param.5) | data formatting | bytes 4194304 | tf_op args[0]
  35.7 16.5 %all-to-all-start = ((bf16[128,16,512]{0,2,1:T(8,128)(2,1)}), bf16[128,16,512]{0,2,1:T(8,128)(2,1)S(1)}, u32[]{:S(2)}, u32[]{:S(2)}) async-start(bf16[128,16,512]{0,2,1:T(8,128)(2,1)} %bitcast.62), calls=%async_computation | async-start | bytes 4194304 | tf_op jit(solution)/shard_map/all_to_all | solution.py:73
  52.2 0.2 multiply_select_fusion
  52.8 0.2 add_select_fusion
  53.0 0.2 copy.82
  53.3 69.3 %all-to-all-done = bf16[128,16,512]{0,2,1:T(8,128)(2,1)S(1)} async-done(((bf16[128,16,512]{0,2,1:T(8,128)(2,1)}), bf16[128,16,512]{0,2,1:T(8,128)(2,1)S(1)}, u32[]{:S(2)}, u32[]{:S(2)}) %all-to-all-start) | async-done | bytes 2097184 | tf_op jit(solution)/shard_map/all_to_all | solution.py:73
  122.6 2.6 %copy.63 = bf16[16,128,512]{2,1,0:T(8,128)(2,1)} copy(bf16[16,128,512]{1,2,0:T(8,128)(2,1)S(1)} %bitcast.61) | data formatting | bytes 4194304 | tf_op jit(solution)/shard_map/all_to_all | solution.py:73
  125.2 5.4 %bitcast_add_fusion = f32[1024,512]{1,0:T(8,128)S(1)} fusion(bf16[1,1024,512]{2,1,0:T(8,128)(2,1)} %param.9, bf16[2048,1024]{1,0:T(8,128)(2,1)} %all-gather.4.cloned.1.call-done, bf16[2048,512]{1,0:T(8,128)(2,1)} %bitcast.63), kind=kOutput, calls=%fused_computation.6 | convolution fusion | flops 2150105088 | bytes 9437184 | tf_op jit(solution)/shard_map/dot_general | solution.py:75
  130.6 3.5 %convolution_bitcast_fusion.2 = f32[16,64,512]{2,1,0:T(8,128)} fusion(f32[16,64,512]{2,1,0:T(8,128)S(1)} %bitcast.60, f32[64]{0:T(128)S(1)} %get-tuple-element.6, f32[64]{0:T(128)S(1)} %get-tuple-element.7, pred[64]{0:T(512)(128)(4,1)S(1)} %iota_compare_fusion.2), kind=kOutput, calls=%fused_computation.10 | convolution fusion | flops 402673664 | bytes 4194880 | tf_op jit(solution)/shard_map/ku,aud->akd/dot_general | solution.py:28
  134.1 2.6 %reshape.310 = f32[4096,128]{1,0:T(8,128)} reshape(f32[16,64,512]{2,1,0:T(8,128)} %convolution_bitcast_fusion.2) | data formatting | bytes 4194304 | tf_op jit(solution)/shard_map/reshape | solution.py:29
  136.8 4.7 %fusion.23 = f32[4096,128]{1,0:T(8,128)} fusion(f32[4096,128]{1,0:T(8,128)} %reshape.310, f32[128,128]{1,0:T(8,128)S(1)} %mul.235), kind=kOutput, calls=%fused_computation.55 | convolution fusion | flops 805306368 | bytes 4259840 | tf_op jit(solution)/shard_map/dot_general | solution.py:30
  141.5 10.6 %reshape_reshape.2 = f32[16,64,32,16]{3,2,1,0:T(8,128)} reshape(f32[4096,128]{1,0:T(8,128)} %fusion.23) | data formatting | bytes 4194304 | tf_op jit(solution)/shard_map/reshape;reshape | solution.py:49
  152.1 11.6 %select_reduce_fusion = f32[16,64,32]{2,1,0:T(8,128)S(1)} fusion(f32[16,64,32,16]{3,2,1,0:T(8,128)} %reshape_reshape.2, s32[16,64,32]{2,1,0:T(8,128)S(1)} %add_select_fusion), kind=kLoop, calls=%fused_computation | loop fusion | flops 1540096 | bytes 2359296 | tf_op jit(solution)/shard_map/reduce_sum | solution.py:50
  164.3 0.8 fusion.4
  165.2 1.1 copy.75
  166.3 6.2 %all_gather.10 = bf16[2,16,64,32]{2,3,1,0:T(8,128)(2,1)S(1)} all-gather(bf16[1,16,64,32]{2,3,1,0:T(8,128)(2,1)S(1)} %copy.75), channel_id=1, replica_groups=mesh['rep'=2,'shard'=16] {'rep'}, dimensions={0}, use_global_device_ids=true | all-gather | bytes 196608 | tf_op jit(solution)/shard_map/all_gather | solution.py:92
  172.5 4.5 %all-gather.1 = bf16[2,16,8]{1,2,0:T(8,128)(2,1)S(1)} all-gather(bf16[1,16,8]{1,2,0:T(8,128)(2,1)S(1)} %get-tuple-element.4), channel_id=2, replica_groups=mesh['rep'=2,'shard'=16] {'rep'}, dimensions={0}, use_global_device_ids=true | all-gather | bytes 768 | tf_op jit(solution)/shard_map/all_gather | solution.py:93
  177.1 0.2 multiply_reduce_fusion
  177.3 2.7 %bitcast_select_fusion = (f32[16,64,512]{1,2,0:T(8,128)}, f32[16,64,512]{1,2,0:T(8,128)S(1)}) fusion(s32[16,64,32]{1,2,0:T(8,128)S(1)} %copy.82, f32[16,64,32]{1,2,0:T(8,128)S(1)} %broadcast_multiply_fusion, s32[512]{0:T(512)S(1)} %eq.87, f32[16,64,32]{1,2,0:T(8,128)S(1)} %convert_multiply_fusion.1), kind=kLoop, calls=%fused_computation.3 | loop fusion | flops 1572864 | bytes 4589568 | tf_op jit(solution)/shard_map/mul | solution.py:54
  180.0 6.4 %convolution_bitcast_fusion.1 = f32[16,64,512]{2,1,0:T(8,128)} fusion(f32[16,64,512]{1,2,0:T(8,128)S(1)} %get-tuple-element.3, f32[64]{0:T(128)S(1)} %get-tuple-element.6, f32[64]{0:T(128)S(1)} %get-tuple-element.7, pred[64]{0:T(512)(128)(4,1)S(1)} %iota_compare_fusion.2), kind=kOutput, calls=%fused_computation.9 | convolution fusion | flops 402673664 | bytes 4194880 | tf_op jit(solution)/shard_map/ku,akd->aud/dot_general | solution.py:35
  186.4 2.6 %reshape.311 = f32[4096,128]{1,0:T(8,128)} reshape(f32[16,64,512]{2,1,0:T(8,128)} %convolution_bitcast_fusion.1) | data formatting | bytes 4194304 | tf_op jit(solution)/shard_map/reshape | solution.py:36
  189.0 4.7 %fusion.24 = f32[4096,128]{1,0:T(8,128)} fusion(f32[4096,128]{1,0:T(8,128)} %reshape.311, f32[128,128]{1,0:T(8,128)S(1)} %mul.235), kind=kOutput, calls=%fused_computation.56 | convolution fusion | flops 805306368 | bytes 4259840 | tf_op jit(solution)/shard_map/dot_general | solution.py:37
  193.7 2.7 %reshape.312 = f32[1024,512]{1,0:T(8,128)} reshape(f32[4096,128]{1,0:T(8,128)} %fusion.24) | data formatting | bytes 4194304 | tf_op jit(solution)/shard_map/reshape | solution.py:37
  196.5 3.1 %fusion = bf16[1,1024,512]{2,1,0:T(8,128)(2,1)} fusion(f32[1024,512]{1,0:T(8,128)S(1)} %bitcast_add_fusion, f32[1024,512]{1,0:T(8,128)} %reshape.312), kind=kLoop, calls=%fused_computation.12 | loop fusion | flops 1048576 | bytes 5242880 | tf_op jit(solution)/shard_map/broadcast_in_dim | solution.py:102
  199.6 5.0 %convolution_bitcast_fusion = f32[16,64,512]{2,1,0:T(8,128)S(1)} fusion(f32[16,64,512]{1,2,0:T(8,128)S(1)} %copy-done, f32[64]{0:T(128)S(1)} %get-tuple-element.6, f32[64]{0:T(128)S(1)} %get-tuple-element.7, pred[64]{0:T(512)(128)(4,1)S(1)} %iota_compare_fusion.2), kind=kOutput, calls=%fused_computation.8 | convolution fusion | flops 402673664 | bytes 4194880 | tf_op jit(solution)/shard_map/ku,akd->aud/dot_general | solution.py:35
  204.6 1.4 reshape.313
  206.0 3.4 %convolution_convert_fusion = bf16[4096,128]{1,0:T(8,128)(2,1)S(1)} fusion(f32[4096,128]{1,0:T(8,128)} %reshape.313, f32[128,128]{1,0:T(8,128)S(1)} %mul.235), kind=kOutput, calls=%fused_computation.2 | convolution fusion | flops 805830656 | bytes 3211264 | tf_op jit(solution)/shard_map/dot_general | solution.py:37
  209.4 1.4 convert_element_type.127
  (28 shorter events, 1.3 us)
Async XLA Ops:
  7.2 118.0 %all-gather.4.cloned.1.call-start = ((), (), s32[]{:S(2)}) async-start(), calls=%async_computation.1 | async-start | bytes 4456448 | tf_op jit(solution)/shard_map/all_gather | solution.py:74
  35.7 17.0 %copy-start.1 = (s32[1,16,8]{1,2,0:T(8,128)S(1)}, s32[1,16,8]{1,2,0:T(8,128)}, u32[]{:S(2)}) copy-start(s32[1,16,8]{1,2,0:T(8,128)} %param.8) | copy-start | bytes 1540
  35.7 86.9 %all-to-all-start = ((bf16[128,16,512]{0,2,1:T(8,128)(2,1)}), bf16[128,16,512]{0,2,1:T(8,128)(2,1)S(1)}, u32[]{:S(2)}, u32[]{:S(2)}) async-start(bf16[128,16,512]{0,2,1:T(8,128)(2,1)} %bitcast.62), calls=%async_computation | async-start | bytes 4194304 | tf_op jit(solution)/shard_map/all_to_all | solution.py:73
  196.5 3.1 %copy-start = (f32[16,64,512]{1,2,0:T(8,128)S(1)}, f32[16,64,512]{1,2,0:T(8,128)}, u32[]{:S(2)}) copy-start(f32[16,64,512]{1,2,0:T(8,128)} %get-tuple-element.2) | copy-start | bytes 6291460
Sparse Core Ops, SparseCore 0:
  31.7 83.2 all-gather.3
where the time goes:
time: 218 us
  waiting for transfers between devices  69.3 us (32%)
  matrix products  33.2 us (15%)
  blocking collectives  31.8 us (15%)
  local copies, waits for them, and re-layouts  30.2 us (14%)
  other arithmetic  22.5 us (10%)
  starting transfers between devices  16.5 us (8%)
  between operations  14.2 us (7%)
    all_to_all x1, waiting for transfers between devices, body(): lax.all_to_all(step_rows, 'shard', split_axis=1, concat_axis=0, tiled=True)  69.3 us
    psum x1, blocking collectives, body(): lengths = lax.psum(jnp.sum(onehot, axis=1), 'shard')  21.1 us
    all_to_all x1, starting transfers between devices, body(): lax.all_to_all(step_rows, 'shard', split_axis=1, concat_axis=0, tiled=True)  16.5 us
    reduce_sum x1, other arithmetic, pack_entries(): return jnp.sum(shaped * selector, axis=-1)  11.6 us
    dot_general x2, matrix products, inverse(): mixed = jnp.einsum('ku,akd->aud', matrix, shaped, precision=PRECISE)  11.4 us
    another operation x1, local copies, waits for them, and re-layouts, pack_entries(): shaped = spectrum.reshape(-1, BLOCK, spectrum.shape[1] // STRIDE, STRIDE)  10.6 us
    dot_general x2, matrix products, inverse(): return jnp.dot(flat, matrix_pair, precision=PRECISE).reshape(spectrum.shape)  8.09 us
    all_gather x1, blocking collectives, body(): gathered_values = lax.all_gather(quantized[None], 'rep', axis=0, tiled=True)  6.18 us
  transfers between devices with their start and end apart: 2, of which 1 were waited for; matrix products, arithmetic and copies ran while one was open for 4% of the time, Pallas kernels for 0%

commit v1 on v0

v1 whole, which is shorter than its diff:
```python
import functools
import math

import jax
import jax.numpy as jnp
import numpy as np
from jax import lax
from jax.experimental import pallas as pl
from jax.experimental.pallas import tpu as pltpu
from jax.sharding import PartitionSpec as P

BLOCK = 64
STRIDE = 16
DOCS = 16
LANES = 128

BETA = 0.9
CLIP = 2.0
EPS = 1e-06
MESH = pl.DeviceIdType.MESH
PRECISE = lax.Precision.HIGHEST


def dct_tables():
    freq = np.arange(BLOCK, dtype=np.float64)[:, None]
    place = np.arange(BLOCK, dtype=np.float64)[None, :]
    matrix = np.cos(math.pi * (2.0 * place + 1.0) * freq / (2.0 * BLOCK)) * math.sqrt(2.0 / BLOCK)
    matrix[0] /= math.sqrt(2.0)
    pair = np.kron(np.eye(LANES // BLOCK), matrix).astype(np.float32)
    high = pair.astype(jnp.bfloat16)
    low = (pair - high.astype(np.float32)).astype(jnp.bfloat16)
    return np.stack([high, low, high.T, low.T])


def split(x):
    high = x.astype(jnp.bfloat16)
    return high, (x - high.astype(jnp.float32)).astype(jnp.bfloat16)


def dot32(a, b):
    return jnp.dot(a, b, preferred_element_type=jnp.float32)


def dot3(a, b):
    return dot32(a[0], b[0]) + (dot32(a[0], b[1]) + dot32(a[1], b[0]))


def kernel(
    n, reps, feat, grads, ids, offsets, momentum, tables, res_out, upd_out,
    cols_in, grads_in, grads_t, ids_in, weights, mom_in, tab, moment, dec, dec_in, res_buf, upd_buf,
    loc_sem, ids_send, ids_recv, g_send, g_recv, f_send, f_recv, d_send, d_recv, o_sem,
):
    me = lax.axis_index("shard")
    my_rep = lax.axis_index("rep")
    chunks, _, width = cols_in.shape
    tokens = feat.shape[0]
    panel = grads.shape[1]
    row_width = chunks * width
    cores = 2 if n % 2 == 0 else 1
    sides = 2 if n % 4 == 0 else 1
    depth = n // (cores * sides)
    c = lax.rem(me, cores)
    y = lax.rem(lax.div(me, cores), sides)
    z = lax.div(me, cores * sides)

    def index(zz, yy, cc):
        return (zz * sides + yy) * cores + cc

    def token_rows(j):
        return pl.ds(pl.multiple_of(j * tokens, tokens), tokens)

    barrier = pltpu.get_barrier_semaphore()

    def greet(d, carry):
        pl.semaphore_signal(
            barrier, inc=1, device_id={"shard": lax.rem(me + d, n)}, device_id_type=MESH
        )
        return carry

    def greet_rep(d, carry):
        pl.semaphore_signal(
            barrier, inc=1, device_id={"rep": lax.rem(my_rep + d, reps)}, device_id_type=MESH
        )
        return carry

    lax.fori_loop(1, n, greet, 0)
    lax.fori_loop(1, reps, greet_rep, 0)

    local = [
        pltpu.make_async_copy(grads, grads_in.at[token_rows(me)], loc_sem.at[0]),
        pltpu.make_async_copy(ids, ids_in.at[me], loc_sem.at[1]),
        pltpu.make_async_copy(momentum, mom_in, loc_sem.at[2]),
        pltpu.make_async_copy(tables, tab, loc_sem.at[3]),
    ]
    for q in range(chunks):
        local.append(
            pltpu.make_async_copy(
                feat.at[:, pl.ds(pl.multiple_of(me * row_width + q * width, width), width)],
                cols_in.at[q, token_rows(me)],
                loc_sem.at[4 + q],
            )
        )
    for copy in local:
        copy.start()
    pl.semaphore_wait(barrier, n - 1 + reps - 1)

    def ids_copy(d):
        return pltpu.make_async_remote_copy(
            ids, ids_in.at[me], ids_send.at[d], ids_recv.at[me],
            device_id={"shard": lax.rem(me + d, n)}, device_id_type=MESH,
        )

    def grad_copy(j, slot, target, own=False):
        return pltpu.make_async_remote_copy(
            grads if own else grads_in.at[token_rows(j)],
            grads_in.at[token_rows(j)],
            g_send.at[j, slot],
            g_recv.at[j],
            device_id={"shard": target},
            device_id_type=MESH,
        )

    def feat_copy(q, d):
        target = lax.rem(me + d, n)
        start = pl.multiple_of(target * row_width + q * width, width)
        return pltpu.make_async_remote_copy(
            feat.at[:, pl.ds(start, width)],
            cols_in.at[q, token_rows(me)],
            f_send.at[q, d],
            f_recv.at[q, me],
            device_id={"shard": target},
            device_id_type=MESH,
        )

    def start_ids(d, carry):
        ids_copy(d).start()
        return carry

    lax.fori_loop(1, n, start_ids, 0)

    sends = []

    def send(condition, j, slot, target, own=False):
        sends.append((condition, j, slot, target, own))

        @pl.when(condition)
        def _():
            grad_copy(j, slot, target, own).start()

    def send_features(q):
        def step(d, carry):
            feat_copy(q, d).start()
            return carry

        lax.fori_loop(1, n, step, 0)

    def wait_grad(j):
        grad_copy(j, 0, lax.rem(me + 1, n)).wait_recv()

    always = me >= 0
    send(z + 1 < depth, me, 0, index(lax.rem(z + 1, depth), y, c), True)
    send(z >= 1, me, 1, index(lax.rem(z + depth - 1, depth), y, c), True)
    if sides > 1:
        send(always, me, 2, index(z, 1 - y, c), True)
    if cores > 1:
        send(always, me, 3, index(z, y, 1 - c), True)
    send_features(0)

    def from_side(s):
        if sides == 1:
            return
        for sign in (-1, 1) if s else (1,):
            zz = z + sign * s
            inside = (zz >= 0) & (zz < depth)
            j = index(lax.rem(zz + depth, depth), 1 - y, c)

            @pl.when(inside)
            def _():
                wait_grad(j)

            if cores > 1:
                send(inside, j, 3, index(z, y, 1 - c))

    sent = 1
    for s in range(1, depth):
        for sign in (-1, 1):
            zz = z + sign * s
            inside = (zz >= 0) & (zz < depth)
            j = index(lax.rem(zz + depth, depth), y, c)

            @pl.when(inside)
            def _():
                wait_grad(j)

            following = z - sign
            send(
                inside & (following >= 0) & (following < depth), j, 0,
                index(lax.rem(following + depth, depth), y, c),
            )
            if sides > 1:
                send(inside, j, 2, index(z, 1 - y, c))
            if cores > 1:
                send(inside, j, 3, index(z, y, 1 - c))
        from_side(s - 1)
        if sent < chunks:
            send_features(sent)
            sent += 1
    from_side(depth - 1)
    for q in range(sent, chunks):
        send_features(q)

    for copy in local:
        copy.wait()

    def wait_ids(d, carry):
        source = lax.rem(me + d, n)
        pltpu.make_async_remote_copy(
            ids, ids_in.at[source], ids_send.at[d], ids_recv.at[source],
            device_id={"shard": source}, device_id_type=MESH,
        ).wait_recv()
        return carry

    lax.fori_loop(1, n, wait_ids, 0)
    all_ids = ids_in[...]
    weight = jnp.zeros(all_ids.shape, jnp.float32)
    for doc in range(DOCS):
        hit = (all_ids == doc).astype(jnp.float32)
        count = jnp.sum(jnp.sum(hit, axis=2, keepdims=True), axis=0, keepdims=True)
        weight = weight + hit / jnp.maximum(count, 1.0)
    weights[...] = weight

    def turn(i, carry):
        group = lax.div(i, cores * (n // cores) // cores)
        j = i if cores == 1 else lax.rem(i, n // cores) * cores + lax.rem(c + group, cores)

        @pl.when(i >= n // cores)
        def _():
            wait_grad(j)

        row = weights[j]
        for first in range(0, panel, LANES):
            part = grads_in[token_rows(j), first : first + LANES].astype(jnp.float32)
            grads_t[first : first + LANES, token_rows(j)] = (part.T * row).astype(jnp.bfloat16)
        return carry

    lax.fori_loop(0, n, turn, 0)

    forward_pair = (tab[0], tab[1])
    inverse_pair = (tab[2], tab[3])
    folds = panel // STRIDE
    per_tile = LANES // STRIDE
    tall = BLOCK // STRIDE
    tiles = panel // LANES
    row_sum = (
        lax.broadcasted_iota(jnp.int32, (folds, folds), 0) // tall
        == lax.broadcasted_iota(jnp.int32, (folds, folds), 1) // tall
    ).astype(jnp.float32)
    lane_sum = (
        lax.broadcasted_iota(jnp.int32, (width, width), 0) // BLOCK
        == lax.broadcasted_iota(jnp.int32, (width, width), 1) // BLOCK
    ).astype(jnp.float32)
    residue = (
        lax.broadcasted_iota(jnp.int32, (STRIDE, width), 0)
        + lax.broadcasted_iota(jnp.int32, (STRIDE, width), 1)
    ) % STRIDE

    def mask_of(q, tile):
        rows = []
        for a in range(tile * LANES // BLOCK, (tile + 1) * LANES // BLOCK):
            hit = residue == offsets[q, a : a + 1, :]
            rows += [hit.astype(jnp.float32)] * tall
        return jnp.concatenate(rows, axis=0)

    def spread(values, mask):
        tall_values = jnp.broadcast_to(values[:, None, :], (per_tile, STRIDE, width))
        return tall_values.reshape(LANES, width) * mask

    def invert(values, mask):
        mixed = dot3(inverse_pair, split(spread(values, mask)))
        return dot3(split(mixed), forward_pair)

    def out_copy(q, which):
        return pltpu.make_async_copy(
            (res_buf, upd_buf)[which].at[q],
            (res_out, upd_out)[which].at[:, pl.ds(pl.multiple_of(q * width, width), width)],
            o_sem.at[which, q],
        )

    def dec_copy(q, d):
        return pltpu.make_async_remote_copy(
            dec.at[q], dec_in.at[q, my_rep], d_send.at[q, d], d_recv.at[q, my_rep],
            device_id={"rep": lax.rem(my_rep + d, reps)}, device_id_type=MESH,
        )

    def first_half(q, carry):
        def wait_feat(d, inner):
            source = lax.rem(me + d, n)
            pltpu.make_async_remote_copy(
                feat.at[:, pl.ds(0, width)], cols_in.at[q, token_rows(source)],
                f_send.at[q, d], f_recv.at[q, source],
                device_id={"shard": source}, device_id_type=MESH,
            ).wait_recv()
            return inner

        lax.fori_loop(1, n, wait_feat, 0)
        lanes = pl.ds(pl.multiple_of(q * width, width), width)
        folded = []
        for tile in range(tiles):
            rows = slice(tile * LANES, (tile + 1) * LANES)
            gradient = dot32(grads_t[rows, :], cols_in[q]).astype(jnp.bfloat16).astype(jnp.float32)
            mom = BETA * mom_in[rows, lanes].astype(jnp.float32) + gradient
            moment[rows, :] = mom
            mixed = dot3(forward_pair, split(mom))
            spectrum = dot3(split(mixed), inverse_pair)
            chosen = (spectrum * mask_of(q, tile)).reshape(per_tile, STRIDE, width)
            folded.append(jnp.sum(chosen, axis=1))
        packed = jnp.concatenate(folded, axis=0)
        total = jnp.dot(row_sum, packed * packed, precision=PRECISE, preferred_element_type=jnp.float32)
        total = jnp.dot(total, lane_sum, precision=PRECISE, preferred_element_type=jnp.float32)
        mean_square = total / (BLOCK * tall)
        scale = (CLIP * jnp.sqrt(mean_square + EPS)).astype(jnp.bfloat16).astype(jnp.float32)
        quantized = jnp.clip(packed / scale, -1.0, 1.0).astype(jnp.bfloat16)
        decoded = quantized.astype(jnp.float32) * scale
        dec[q] = decoded

        def start_dec(d, inner):
            dec_copy(q, d).start()
            return inner

        lax.fori_loop(1, reps, start_dec, 0)
        for tile in range(tiles):
            rows = slice(tile * LANES, (tile + 1) * LANES)
            part = decoded[tile * per_tile : (tile + 1) * per_tile]
            back = invert(part, mask_of(q, tile))
            res_buf[q, rows, :] = (moment[rows, :] - back).astype(jnp.bfloat16)
        out_copy(q, 0).start()

        def wait_dec(d, inner):
            source = lax.rem(my_rep + d, reps)
            pltpu.make_async_remote_copy(
                dec.at[q], dec_in.at[q, source], d_send.at[q, d], d_recv.at[q, source],
                device_id={"rep": source}, device_id_type=MESH,
            ).wait_recv()
            return inner + dec_in[q, source]

        average = lax.fori_loop(1, reps, wait_dec, decoded) / reps
        for tile in range(tiles):
            rows = slice(tile * LANES, (tile + 1) * LANES)
            part = average[tile * per_tile : (tile + 1) * per_tile]
            upd_buf[q, rows, :] = invert(part, mask_of(q, tile)).astype(jnp.bfloat16)
        out_copy(q, 1).start()
        return carry

    lax.fori_loop(0, chunks, first_half, 0)

    def drain(q, carry):
        def sent_feat(d, inner):
            feat_copy(q, d).wait_send()
            return inner

        def sent_dec(d, inner):
            dec_copy(q, d).wait_send()
            return inner

        lax.fori_loop(1, n, sent_feat, 0)
        lax.fori_loop(1, reps, sent_dec, 0)
        out_copy(q, 0).wait()
        out_copy(q, 1).wait()
        return carry

    def sent_ids(d, carry):
        ids_copy(d).wait_send()
        return carry

    lax.fori_loop(1, n, sent_ids, 0)
    for condition, j, slot, target, own in sends:

        @pl.when(condition)
        def _():
            grad_copy(j, slot, target, own).wait_send()

    lax.fori_loop(0, chunks, drain, 0)


def body(n, reps, features, out_grads, doc_ids, offsets, momentum):
    feat = features[0, 0]
    grads = out_grads[0, 0]
    tokens, model = feat.shape
    panel = grads.shape[1]
    row_width = momentum.shape[2]
    width = LANES
    chunks = row_width // width
    wide = jnp.repeat(offsets[0], BLOCK, axis=1).reshape(panel // BLOCK, chunks, width)
    wide = jnp.transpose(wide, (1, 0, 2))
    folds = panel // STRIDE
    anywhere = pl.BlockSpec(memory_space=pl.ANY)
    vmem = pl.BlockSpec(memory_space=pltpu.VMEM)
    dma = pltpu.SemaphoreType.DMA
    residual, update = pl.pallas_call(
        functools.partial(kernel, n, reps),
        out_shape=(
            jax.ShapeDtypeStruct((panel, row_width), jnp.bfloat16),
            jax.ShapeDtypeStruct((panel, row_width), jnp.bfloat16),
        ),
        in_specs=[anywhere, anywhere, vmem, vmem, anywhere, anywhere],
        out_specs=(anywhere, anywhere),
        scratch_shapes=[
            pltpu.VMEM((chunks, n * tokens, width), jnp.bfloat16),
            pltpu.VMEM((n * tokens, panel), jnp.bfloat16),
            pltpu.VMEM((panel, n * tokens), jnp.bfloat16),
            pltpu.VMEM((n, 1, tokens), jnp.int32),
            pltpu.VMEM((n, 1, tokens), jnp.float32),
            pltpu.VMEM((panel, row_width), jnp.bfloat16),
            pltpu.VMEM((4, LANES, LANES), jnp.bfloat16),
            pltpu.VMEM((panel, width), jnp.float32),
            pltpu.VMEM((chunks, folds, width), jnp.float32),
            pltpu.VMEM((chunks, reps, folds, width), jnp.float32),
            pltpu.VMEM((chunks, panel, width), jnp.bfloat16),
            pltpu.VMEM((chunks, panel, width), jnp.bfloat16),
            dma((4 + chunks,)),
            dma((n,)),
            dma((n,)),
            dma((n, 4)),
            dma((n,)),
            dma((chunks, n)),
            dma((chunks, n)),
            dma((chunks, reps)),
            dma((chunks, reps)),
            dma((2, chunks)),
        ],
        compiler_params=pltpu.CompilerParams(collective_id=0, has_side_effects=True),
    )(feat, grads, doc_ids[0], wide, momentum[0], jnp.asarray(dct_tables()))
    return residual[None], update[None]


def solution(mesh):
    return jax.shard_map(
        functools.partial(body, mesh.shape["shard"], mesh.shape["rep"]),
        mesh=mesh,
        in_specs=(
            P(None, "rep", "shard", None),
            P(None, "rep", "shard", None),
            P(None, "rep", "shard"),
            P(None, None, "shard"),
            P("rep", None, "shard"),
        ),
        out_specs=(P("rep", None, "shard"), P(None, None, "shard")),
        check_vma=False,
    )
```

time: 218 us -> 111 us (0.51)
  the two profiles are of different devices: /device:TPU:14 before, /device:TPU:0 now
where the time goes in v1:
time: 111 us
  Pallas kernels  105 us (95%)
  local copies, waits for them, and re-layouts  4.87 us (4%)
    pallas_call x1, Pallas kernels, body(): pl.pallas_call(functools.partial(kernel, n, reps), out_shape=(jax.ShapeDt...  105 us
    unnamed x4, local copies, waits for them, and re-layouts  3.32 us

profile of v1, /device:TPU:0, one launch (start us, length us, event | category | flops | bytes accessed | tf_op | source)
XLA Modules:
  0.0 110.6 jit_solution(9138344675521843956)
XLA Ops:
  0.6 0.8 copy.9
  1.4 0.1 broadcast_in_dim.9
  1.5 0.1 reshape_reshape.3
  1.6 0.6 copy.12
  2.2 105.1 %shard_map.77 = (bf16[1024,512]{1,0:T(8,128)(2,1)}, bf16[1024,512]{1,0:T(8,128)(2,1)}) custom-call(bf16[128,8192]{1,0:T(8,128)(2,1)} %bitcast.10, bf16[128,1024]{1,0:T(8,128)(2,1)} %bitcast.14, s32[1,128]{1,0:T(1,128)} %bitcast.17, s32[4,16,128]{2,1,0:T(8,128)} %bitcast.15, bf16[1024,512]{1,0:T(8,128)(2,1)} %bitcast.13, ...), custom_call_target="tpu_custom_call" | custom-call | tf_op jit(solution)/shard_map/pallas_call | solution.py:399
  107.3 0.0 copy-start
  107.3 2.4 %copy.15 = bf16[1,1024,512]{2,1,0:T(8,128)(2,1)} copy(bf16[1,1024,512]{2,1,0:T(8,128)(2,1)} %bitcast.12) | data formatting | bytes 2097152
  109.6 0.0 copy-done
  109.6 1.0 copy.16
Async XLA Ops:
  107.3 2.4 %copy-start = (bf16[1024,512]{1,0:T(8,128)(2,1)S(1)}, bf16[1024,512]{1,0:T(8,128)(2,1)}, u32[]{:S(2)}) copy-start(bf16[1024,512]{1,0:T(8,128)(2,1)} %get-tuple-element.5) | copy-start | bytes 3145732

commit v2 on v1

--- a/solution.py
+++ b/solution.py
@@ -29,7 +29,10 @@
     pair = np.kron(np.eye(LANES // BLOCK), matrix).astype(np.float32)
     high = pair.astype(jnp.bfloat16)
     low = (pair - high.astype(np.float32)).astype(jnp.bfloat16)
-    return np.stack([high, low, high.T, low.T])
+    zero = np.zeros_like(high)
+    left = [np.concatenate([high, low]), np.concatenate([high.T, low.T])]
+    right = [np.block([[high.T, low.T], [high.T, zero]]), np.block([[high, low], [high, zero]])]
+    return np.stack(left), np.stack(right)
 
 
 def split(x):
@@ -41,13 +44,9 @@
     return jnp.dot(a, b, preferred_element_type=jnp.float32)
 
 
-def dot3(a, b):
-    return dot32(a[0], b[0]) + (dot32(a[0], b[1]) + dot32(a[1], b[0]))
-
-
 def kernel(
-    n, reps, feat, grads, ids, offsets, momentum, tables, res_out, upd_out,
-    cols_in, grads_in, grads_t, ids_in, weights, mom_in, tab, moment, dec, dec_in, res_buf, upd_buf,
+    n, reps, feat, grads, ids, offsets, momentum, left, right, res_out, upd_out,
+    cols_in, grads_in, grads_t, ids_in, weights, mom_in, tab_l, tab_r, wide, moment, mix, dec, dec_in, res_buf, upd_buf,
     loc_sem, ids_send, ids_recv, g_send, g_recv, f_send, f_recv, d_send, d_recv, o_sem,
 ):
     me = lax.axis_index("shard")
@@ -90,14 +89,15 @@
         pltpu.make_async_copy(grads, grads_in.at[token_rows(me)], loc_sem.at[0]),
         pltpu.make_async_copy(ids, ids_in.at[me], loc_sem.at[1]),
         pltpu.make_async_copy(momentum, mom_in, loc_sem.at[2]),
-        pltpu.make_async_copy(tables, tab, loc_sem.at[3]),
+        pltpu.make_async_copy(left, tab_l, loc_sem.at[3]),
+        pltpu.make_async_copy(right, tab_r, loc_sem.at[4]),
     ]
     for q in range(chunks):
         local.append(
             pltpu.make_async_copy(
                 feat.at[:, pl.ds(pl.multiple_of(me * row_width + q * width, width), width)],
                 cols_in.at[q, token_rows(me)],
-                loc_sem.at[4 + q],
+                loc_sem.at[5 + q],
             )
         )
     for copy in local:
@@ -164,8 +164,6 @@
         send(always, me, 2, index(z, 1 - y, c), True)
     if cores > 1:
         send(always, me, 3, index(z, y, 1 - c), True)
-    send_features(0)
-
     def from_side(s):
         if sides == 1:
             return
@@ -181,7 +179,7 @@
             if cores > 1:
                 send(inside, j, 3, index(z, y, 1 - c))
 
-    sent = 1
+    sent = 0
     for s in range(1, depth):
         for sign in (-1, 1):
             zz = z + sign * s
@@ -202,12 +200,21 @@
             if cores > 1:
                 send(inside, j, 3, index(z, y, 1 - c))
         from_side(s - 1)
-        if sent < chunks:
-            send_features(sent)
-            sent += 1
+        for q in range(sent, min(chunks, (s >= depth // 2) + chunks * (s > depth // 2))):
+            send_features(q)
+            sent = q + 1
     from_side(depth - 1)
     for q in range(sent, chunks):
         send_features(q)
+
+    own_blocks = offsets.shape[0]
+    for q in range(chunks):
+        block_of = (lax.broadcasted_iota(jnp.int32, (own_blocks, width), 1) + q * width) // BLOCK
+        pick = (block_of == lax.broadcasted_iota(jnp.int32, (own_blocks, width), 0)).astype(jnp.float32)
+        wide[q] = lax.dot_general(
+            offsets[...].astype(jnp.float32), pick, (((0,), (0,)), ((), ())),
+            precision=PRECISE, preferred_element_type=jnp.float32,
+        ).astype(jnp.int32)
 
     for copy in local:
         copy.wait()
@@ -245,8 +252,6 @@
 
     lax.fori_loop(0, n, turn, 0)
 
-    forward_pair = (tab[0], tab[1])
-    inverse_pair = (tab[2], tab[3])
     folds = panel // STRIDE
     per_tile = LANES // STRIDE
     tall = BLOCK // STRIDE
@@ -267,7 +272,7 @@
     def mask_of(q, tile):
         rows = []
         for a in range(tile * LANES // BLOCK, (tile + 1) * LANES // BLOCK):
-            hit = residue == offsets[q, a : a + 1, :]
+            hit = residue == wide[q, a : a + 1, :]
             rows += [hit.astype(jnp.float32)] * tall
         return jnp.concatenate(rows, axis=0)
 
@@ -275,9 +280,22 @@
         tall_values = jnp.broadcast_to(values[:, None, :], (per_tile, STRIDE, width))
         return tall_values.reshape(LANES, width) * mask
 
-    def invert(values, mask):
-        mixed = dot3(inverse_pair, split(spread(values, mask)))
-        return dot3(split(mixed), forward_pair)
+    def mix_rows(tile, values, way):
+        both = dot32(tab_l[way], jnp.concatenate(split(values), axis=1))
+        mixed = both[:LANES, :width] + (both[:LANES, width:] + both[LANES:, :width])
+        high, low = split(mixed)
+        mix[tile * LANES : (tile + 1) * LANES, :width] = high
+        mix[tile * LANES : (tile + 1) * LANES, width:] = low
+
+    def mix_columns(way):
+        both = dot32(mix[...], tab_r[way])
+        return both[:, :width] + both[:, width:]
+
+    def invert(q, values):
+        for tile in range(tiles):
+            part = values[tile * per_tile : (tile + 1) * per_tile]
+            mix_rows(tile, spread(part, mask_of(q, tile)), 1)
+        return mix_columns(1)
 
     def out_copy(q, which):
         return pltpu.make_async_copy(
@@ -291,6 +309,19 @@
             dec.at[q], dec_in.at[q, my_rep], d_send.at[q, d], d_recv.at[q, my_rep],
             device_id={"rep": lax.rem(my_rep + d, reps)}, device_id_type=MESH,
         )
+
+    def finish_update(q):
+        def wait_dec(d, inner):
+            source = lax.rem(my_rep + d, reps)
+            pltpu.make_async_remote_copy(
+                dec.at[q], dec_in.at[q, source], d_send.at[q, d], d_recv.at[q, source],
+                device_id={"rep": source}, device_id_type=MESH,
+            ).wait_recv()
+            return inner + dec_in[q, source]
+
+        average = lax.fori_loop(1, reps, wait_dec, dec[q]) / reps
+        upd_buf[q] = invert(q, average).astype(jnp.bfloat16)
+        out_copy(q, 1).start()
 
     def first_half(q, carry):
         def wait_feat(d, inner):
@@ -304,15 +335,15 @@
 
         lax.fori_loop(1, n, wait_feat, 0)
         lanes = pl.ds(pl.multiple_of(q * width, width), width)
+        gradient = dot32(grads_t[...], cols_in[q]).astype(jnp.bfloat16).astype(jnp.float32)
+        moment[...] = BETA * mom_in[:, lanes].astype(jnp.float32) + gradient
+        for tile in range(tiles):
+            mix_rows(tile, moment[tile * LANES : (tile + 1) * LANES, :], 0)
+        spectrum = mix_columns(0)
         folded = []
         for tile in range(tiles):
             rows = slice(tile * LANES, (tile + 1) * LANES)
-            gradient = dot32(grads_t[rows, :], cols_in[q]).astype(jnp.bfloat16).astype(jnp.float32)
-            mom = BETA * mom_in[rows, lanes].astype(jnp.float32) + gradient
-            moment[rows, :] = mom
-            mixed = dot3(forward_pair, split(mom))
-            spectrum = dot3(split(mixed), inverse_pair)
-            chosen = (spectrum * mask_of(q, tile)).reshape(per_tile, STRIDE, width)
+            chosen = (spectrum[rows] * mask_of(q, tile)).reshape(per_tile, STRIDE, width)
             folded.append(jnp.sum(chosen, axis=1))
         packed = jnp.concatenate(folded, axis=0)
         total = jnp.dot(row_sum, packed * packed, precision=PRECISE, preferred_element_type=jnp.float32)
@@ -328,30 +359,17 @@
             return inner
 
         lax.fori_loop(1, reps, start_dec, 0)
-        for tile in range(tiles):
-            rows = slice(tile * LANES, (tile + 1) * LANES)
-            part = decoded[tile * per_tile : (tile + 1) * per_tile]
-            back = invert(part, mask_of(q, tile))
-            res_buf[q, rows, :] = (moment[rows, :] - back).astype(jnp.bfloat16)
+        res_buf[q] = (moment[...] - invert(q, decoded)).astype(jnp.bfloat16)
         out_copy(q, 0).start()
 
-        def wait_dec(d, inner):
-            source = lax.rem(my_rep + d, reps)
-            pltpu.make_async_remote_copy(
-                dec.at[q], dec_in.at[q, source], d_send.at[q, d], d_recv.at[q, source],
-                device_id={"rep": source}, device_id_type=MESH,
-            ).wait_recv()
-            return inner + dec_in[q, source]
-
-        average = lax.fori_loop(1, reps, wait_dec, decoded) / reps
-        for tile in range(tiles):
-            rows = slice(tile * LANES, (tile + 1) * LANES)
-            part = average[tile * per_tile : (tile + 1) * per_tile]
-            upd_buf[q, rows, :] = invert(part, mask_of(q, tile)).astype(jnp.bfloat16)
-        out_copy(q, 1).start()
+        @pl.when(q > 0)
+        def _():
+            finish_update(q - 1)
+
         return carry
 
     lax.fori_loop(0, chunks, first_half, 0)
+    finish_update(chunks - 1)
 
     def drain(q, carry):
         def sent_feat(d, inner):
@@ -390,8 +408,6 @@
     row_width = momentum.shape[2]
     width = LANES
     chunks = row_width // width
-    wide = jnp.repeat(offsets[0], BLOCK, axis=1).reshape(panel // BLOCK, chunks, width)
-    wide = jnp.transpose(wide, (1, 0, 2))
     folds = panel // STRIDE
     anywhere = pl.BlockSpec(memory_space=pl.ANY)
     vmem = pl.BlockSpec(memory_space=pltpu.VMEM)
@@ -402,7 +418,7 @@
             jax.ShapeDtypeStruct((panel, row_width), jnp.bfloat16),
             jax.ShapeDtypeStruct((panel, row_width), jnp.bfloat16),
         ),
-        in_specs=[anywhere, anywhere, vmem, vmem, anywhere, anywhere],
+        in_specs=[anywhere, anywhere, vmem, vmem, anywhere, anywhere, anywhere],
         out_specs=(anywhere, anywhere),
         scratch_shapes=[
             pltpu.VMEM((chunks, n * tokens, width), jnp.bfloat16),
@@ -411,13 +427,16 @@
             pltpu.VMEM((n, 1, tokens), jnp.int32),
             pltpu.VMEM((n, 1, tokens), jnp.float32),
             pltpu.VMEM((panel, row_width), jnp.bfloat16),
-            pltpu.VMEM((4, LANES, LANES), jnp.bfloat16),
+            pltpu.VMEM((2, 2 * LANES, LANES), jnp.bfloat16),
+            pltpu.VMEM((2, 2 * LANES, 2 * width), jnp.bfloat16),
+            pltpu.VMEM((chunks, panel // BLOCK, width), jnp.int32),
             pltpu.VMEM((panel, width), jnp.float32),
+            pltpu.VMEM((panel, 2 * width), jnp.bfloat16),
             pltpu.VMEM((chunks, folds, width), jnp.float32),
             pltpu.VMEM((chunks, reps, folds, width), jnp.float32),
             pltpu.VMEM((chunks, panel, width), jnp.bfloat16),
             pltpu.VMEM((chunks, panel, width), jnp.bfloat16),
-            dma((4 + chunks,)),
+            dma((5 + chunks,)),
             dma((n,)),
             dma((n,)),
             dma((n, 4)),
@@ -429,7 +448,7 @@
             dma((2, chunks)),
         ],
         compiler_params=pltpu.CompilerParams(collective_id=0, has_side_effects=True),
-    )(feat, grads, doc_ids[0], wide, momentum[0], jnp.asarray(dct_tables()))
+    )(feat, grads, doc_ids[0], offsets[0].T, momentum[0], *map(jnp.asarray, dct_tables()))
     return residual[None], update[None]
 
 

time: 111 us -> 83 us (0.75)
  the two profiles are of different devices: /device:TPU:0 before, /device:TPU:29 now
where the time goes in v2:
time: 83 us; the launch traced here: 82.8 us
  Pallas kernels  78.9 us (95%)
  local copies, waits for them, and re-layouts  3.32 us (4%)
    pallas_call x1, Pallas kernels, body(): pl.pallas_call(functools.partial(kernel, n, reps), out_shape=(jax.ShapeDt...  78.9 us
    unnamed x4, local copies, waits for them, and re-layouts  3.32 us

profile of v2, /device:TPU:29, one launch (start us, length us, event | category | flops | bytes accessed | tf_op | source)
XLA Modules:
  0.0 82.8 jit_solution(14543893168557549920)
XLA Ops:
  0.6 78.9 %shard_map.86 = (bf16[1024,512]{1,0:T(8,128)(2,1)}, bf16[1024,512]{1,0:T(8,128)(2,1)}) custom-call(bf16[128,8192]{1,0:T(8,128)(2,1)} %bitcast.9, bf16[128,1024]{1,0:T(8,128)(2,1)} %bitcast.13, s32[1,128]{1,0:T(1,128)} %bitcast.15, s32[8,16]{1,0:T(8,128)} %bitcast.14, bf16[1024,512]{1,0:T(8,128)(2,1)} %bitcast.10, bf16[2,256,128]{2,1,0:T(8,128)(2,1)} %constant.4.clone.left, ...), custom_call_target="tpu_custom_call" | custom-call | tf_op jit(solution)/shard_map/pallas_call | solution.py:415
  79.5 0.0 copy-start
  79.5 2.4 %copy.11 = bf16[1,1024,512]{2,1,0:T(8,128)(2,1)} copy(bf16[1,1024,512]{2,1,0:T(8,128)(2,1)} %bitcast.12) | data formatting | bytes 2097152
  81.9 0.0 copy-done
  81.9 1.0 %copy.12 = bf16[1,1024,512]{2,1,0:T(8,128)(2,1)} copy(bf16[1,1024,512]{2,1,0:T(8,128)(2,1)S(1)} %bitcast.11) | data formatting | bytes 2097152
Async XLA Ops:
  79.5 2.4 %copy-start = (bf16[1024,512]{1,0:T(8,128)(2,1)S(1)}, bf16[1024,512]{1,0:T(8,128)(2,1)}, u32[]{:S(2)}) copy-start(bf16[1024,512]{1,0:T(8,128)(2,1)} %get-tuple-element.5) | copy-start | bytes 3145732

commit v3 on v2

--- a/solution.py
+++ b/solution.py
@@ -199,11 +199,12 @@
                 send(inside, j, 2, index(z, 1 - y, c))
             if cores > 1:
                 send(inside, j, 3, index(z, y, 1 - c))
-        from_side(s - 1)
-        for q in range(sent, min(chunks, (s >= depth // 2) + chunks * (s > depth // 2))):
+        due = (chunks + 1) // 2 if s == depth // 2 else chunks if s > depth // 2 else 0
+        for q in range(sent, due):
             send_features(q)
             sent = q + 1
-    from_side(depth - 1)
+    for s in range(depth):
+        from_side(s)
     for q in range(sent, chunks):
         send_features(q)
 

time: 83 us -> 81.5 us (0.982)
  the two profiles are of different devices: /device:TPU:29 before, /device:TPU:0 now
where the time goes in v3:
time: 81.5 us; the launch traced here: 81.3 us
  Pallas kernels  77.3 us (95%)
  local copies, waits for them, and re-layouts  3.32 us (4%)
    pallas_call x1, Pallas kernels, body(): pl.pallas_call(functools.partial(kernel, n, reps), out_shape=(jax.ShapeDt...  77.3 us
    unnamed x4, local copies, waits for them, and re-layouts  3.32 us

profile of v3, /device:TPU:0, one launch (start us, length us, event | category | flops | bytes accessed | tf_op | source)
XLA Modules:
  0.0 81.3 jit_solution(4758993052924735451)
XLA Ops:
  0.6 77.3 %shard_map.86 = (bf16[1024,512]{1,0:T(8,128)(2,1)}, bf16[1024,512]{1,0:T(8,128)(2,1)}) custom-call(bf16[128,8192]{1,0:T(8,128)(2,1)} %bitcast.9, bf16[128,1024]{1,0:T(8,128)(2,1)} %bitcast.13, s32[1,128]{1,0:T(1,128)} %bitcast.15, s32[8,16]{1,0:T(8,128)} %bitcast.14, bf16[1024,512]{1,0:T(8,128)(2,1)} %bitcast.10, bf16[2,256,128]{2,1,0:T(8,128)(2,1)} %constant.4.clone.left, ...), custom_call_target="tpu_custom_call" | custom-call | tf_op jit(solution)/shard_map/pallas_call | solution.py:416
  78.0 0.0 copy-start
  78.0 2.4 %copy.11 = bf16[1,1024,512]{2,1,0:T(8,128)(2,1)} copy(bf16[1,1024,512]{2,1,0:T(8,128)(2,1)} %bitcast.12) | data formatting | bytes 2097152
  80.3 0.0 copy-done
  80.3 1.0 %copy.12 = bf16[1,1024,512]{2,1,0:T(8,128)(2,1)} copy(bf16[1,1024,512]{2,1,0:T(8,128)(2,1)S(1)} %bitcast.11) | data formatting | bytes 2097152
Async XLA Ops:
  78.0 2.4 %copy-start = (bf16[1024,512]{1,0:T(8,128)(2,1)S(1)}, bf16[1024,512]{1,0:T(8,128)(2,1)}, u32[]{:S(2)}) copy-start(bf16[1024,512]{1,0:T(8,128)(2,1)} %get-tuple-element.5) | copy-start | bytes 3145732
